TPU v7x, 256 devices: a whole 4x4x8 slice. The times are simulated.
256 devices in a mesh: seq: 64 (over x, z_hi, y), heads: 4 (over z_lo, core).
Axes of the slice: x: 4, y: 4, z: 8 (z_hi: 4, z_lo: 2; z = z_hi * 2 + z_lo), core: 2. Of those that a mesh axis runs over, the one named last changes fastest.
Arguments:
- queries: bfloat16 [131072, 2048], P('seq', 'heads'), may hold values from -120 to 120
- keys: bfloat16 [512, 2048], P(None, 'heads'), may hold values from -4.2 to 4.2
- values: bfloat16 [512, 2048], P(None, 'heads'), may hold values from -6 to 6
- out_grad: bfloat16 [131072, 2048], P('seq', 'heads'), may hold values from -6 to 6
- key_proj: bfloat16 [2048, 2048], P(None, 'heads'), may hold values from -0.125 to 0.125
- value_proj: bfloat16 [2048, 2048], P(None, 'heads'), may hold values from -0.125 to 0.125
- global_in: bfloat16 [512, 2048], P('seq', 'heads'), may hold values from -6 to 6
- up_proj: bfloat16 [2048, 8192], P('heads', 'seq'), may hold values from -0.125 to 0.125
- down_proj: bfloat16 [8192, 2048], P('seq', 'heads'), may hold values from -0.0625 to 0.0625
Outputs:
- query_grad: bfloat16 [131072, 2048], P('seq', 'heads')
- global_grad: float32 [512, 2048], P('seq', 'heads')
All inputs are finite; a program needn't handle non-finite values.
Results may differ from a plain program's by a relative error of at most 0.014.
Values may be sent and summed in bfloat16 or wider, within the bound.
A program may use at most 128 MiB of HBM per device.

v0:
```python
import jax
import jax.numpy as jnp
from jax import lax
from jax.sharding import PartitionSpec as P

HD = 128


def slope_of(pre):
    return (
        0.5 * (1.0 + lax.erf(pre * 0.7071067811865476))
        + pre * jnp.exp(-0.5 * pre * pre) * 0.3989422804014327
    )


def project(key_sum, value_sum, key_proj, value_proj):
    first = jnp.einsum(
        "gc,dc->gd", key_sum.astype(jnp.bfloat16), key_proj, preferred_element_type=jnp.float32
    )
    second = jnp.einsum(
        "gc,dc->gd", value_sum.astype(jnp.bfloat16), value_proj, preferred_element_type=jnp.float32
    )
    return first + second


def local(queries, keys, values, out_grad, key_proj, value_proj, global_in, up_proj, down_proj):
    tok_rows, width = queries.shape
    glob_rows = keys.shape[0]
    local_heads = width // HD
    scale = HD ** (-0.5)
    block = min(512, tok_rows)
    blocks = tok_rows // block
    pre_part = jnp.dot(
        lax.all_gather(global_in, "seq", axis=0, tiled=True),
        up_proj,
        preferred_element_type=jnp.float32,
    )
    key_heads = keys.reshape(glob_rows, local_heads, HD)
    value_heads = values.reshape(glob_rows, local_heads, HD)
    query_blocks = queries.reshape(blocks, block, local_heads, HD)
    grad_blocks = out_grad.reshape(blocks, block, local_heads, HD)

    def attend(carry, pair):
        key_total, value_total = carry
        query_block, grad_block = pair
        scores = scale * jnp.einsum(
            "rhd,ghd->hrg", query_block, key_heads, preferred_element_type=jnp.float32
        )
        weights = jax.nn.softmax(scores, axis=-1)
        weight_grad = jnp.einsum(
            "rhd,ghd->hrg", grad_block, value_heads, preferred_element_type=jnp.float32
        )
        centre = jnp.sum(weights * weight_grad, axis=-1, keepdims=True)
        score_grad = (weights * (weight_grad - centre)).astype(jnp.bfloat16)
        weights_low = weights.astype(jnp.bfloat16)
        block_grad = (
            scale
            * jnp.einsum("hrg,ghd->rhd", score_grad, key_heads, preferred_element_type=jnp.float32)
        ).astype(jnp.bfloat16)
        key_total = key_total + jnp.einsum(
            "hrg,rhd->ghd", score_grad, query_block, preferred_element_type=jnp.float32
        )
        value_total = value_total + jnp.einsum(
            "hrg,rhd->ghd", weights_low, grad_block, preferred_element_type=jnp.float32
        )
        return ((key_total, value_total), block_grad)

    empty = jnp.zeros((glob_rows, local_heads, HD), jnp.float32)
    (key_total, value_total), block_grads = lax.scan(
        attend, (empty, empty), (query_blocks, grad_blocks)
    )
    query_grad = block_grads.reshape(tok_rows, width)
    key_total = scale * key_total.reshape(glob_rows, width)
    value_total = value_total.reshape(glob_rows, width)
    key_sum, value_sum = lax.psum((key_total, value_total), "seq")
    state_share = lax.psum_scatter(
        project(key_sum, value_sum, key_proj, value_proj).astype(jnp.bfloat16),
        "heads",
        scatter_dimension=1,
        tiled=True,
    ).astype(jnp.float32)
    state_low = state_share.astype(jnp.bfloat16)
    share_rows = glob_rows // lax.axis_size("seq")
    own_state = lax.dynamic_slice_in_dim(
        state_share, lax.axis_index("seq") * share_rows, share_rows, 0
    )
    back_part = jnp.einsum("gc,fc->gf", state_low, down_proj, preferred_element_type=jnp.float32)
    pre_total, back_total = (
        lax.psum(pre_part.astype(jnp.bfloat16), "heads").astype(jnp.float32),
        lax.psum(back_part.astype(jnp.bfloat16), "heads").astype(jnp.float32),
    )
    gated = (slope_of(pre_total) * back_total).astype(jnp.bfloat16)
    input_part = jnp.einsum("gf,cf->gc", gated, up_proj, preferred_element_type=jnp.float32)
    global_grad = own_state + lax.psum_scatter(input_part, "seq", scatter_dimension=0, tiled=True)
    return (query_grad, global_grad)


def solution(mesh):
    placed = (
        P("seq", "heads"),
        P(None, "heads"),
        P(None, "heads"),
        P("seq", "heads"),
        P(None, "heads"),
        P(None, "heads"),
        P("seq", "heads"),
        P("heads", "seq"),
        P("seq", "heads"),
    )
    return jax.shard_map(
        local,
        mesh=mesh,
        in_specs=placed,
        out_specs=(P("seq", "heads"), P("seq", "heads")),
        check_vma=False,
    )
```

profile of v0, /device:TPU:0, one launch (start us, length us, event | category | flops | bytes accessed | tf_op | source)
XLA Modules:
  0.0 1139.3 jit_solution(193295031529866412)
XLA Ops:
  11.2 4.0 reshape.28
  15.2 4.0 reshape.30
  19.2 83.3 %while.15 = (s32[]{:T(128)}, f32[512,4,128]{0,2,1:T(8,128)}, f32[512,4,128]{0,2,1:T(8,128)}, bf16[4,512,4,128]{3,2,1,0:T(4,128)(2,1)}, bf16[4,512,4,128]{3,2,1,0...) while((s32[]{:T(128)}, f32[512,4,128]{0,2,1:T(8,128)}, ...), condition=%wide.region_4.5_spmd.clone, body=%wide.region_0.4_spmd.clone.sunk | while | flops 1360528384 | bytes 93372648 | solution.py:69
  22.3 3.2 fusion.82
  25.5 6.4 fusion.84
  31.8 3.4 multiply_reduce_fusion.3
  39.9 2.4 constant_dynamic-slice_fusion.3
  43.0 3.2 fusion.82
  46.1 6.6 fusion.84
  52.7 3.4 multiply_reduce_fusion.3
  60.7 2.4 constant_dynamic-slice_fusion.3
  63.8 3.2 fusion.82
  67.0 6.6 fusion.84
  73.6 3.4 multiply_reduce_fusion.3
  81.6 2.4 constant_dynamic-slice_fusion.3
  84.7 3.2 fusion.82
  87.9 6.6 fusion.84
  94.4 3.4 multiply_reduce_fusion.3
  104.8 403.6 %all-reduce.6 = (bf16[512,512]{0,1:T(8,128)(2,1)S(1)}, bf16[512,512]{0,1:T(8,128)(2,1)S(1)}) all-reduce(f32[512,512]{0,1:T(8,128)} %bitcast.69, f32[512,512]{0,1:T(8,128)} %bitcast.74), channel_id=1, replica_groups=mesh['seq'=64,'heads'=4] {'seq'}, use_global_device_ids=true, to_apply=%region_5.6 | all-reduce | flops 524288 | bytes 3145728 | tf_op jit(solution)/shard_map/psum | solution.py:75
  510.0 2.6 add_convert_fusion
  512.8 187.2 %all_gather.3 = bf16[512,512]{1,0:T(8,128)(2,1)S(1)} all-gather(bf16[8,512]{1,0:T(8,128)(2,1)S(1)} %copy-done.8), channel_id=1, replica_groups=mesh['seq'=64,'heads'=4] {'seq'}, dimensions={0}, use_global_device_ids=true | all-gather | bytes 532480 | tf_op jit(solution)/shard_map/all_gather | solution.py:34
  702.9 38.1 %all-reduce.5.cloned.1.call-done = (bf16[512,128]{1,0:T(8,128)(2,1)}, bf16[512,128]{1,0:T(8,128)(2,1)}) async-done(((bf16[512,128]{1,0:T(8,128)(2,1)}, bf16[512,128]{1,0:T(8,128)(2,1)}), (bf16[512,128]{1,0:T(8,128)(2,1)}, bf16[512,128]{1,0:T(8,128)(2,1)})) %all-reduce.5.cloned.1.call-update) | async-done | bytes 262160 | tf_op jit(solution)/shard_map/psum | solution.py:90
  743.3 3.3 copy.49
  746.6 384.8 %reduce-scatter.5.cloned.1.call-done = f32[8,512]{1,0:T(8,128)} async-done(((f32[512,512]{1,0:T(8,128)}), f32[8,512]{1,0:T(8,128)}) %reduce-scatter.5.cloned.1.call-update) | async-done | bytes 16400 | tf_op jit(solution)/shard_map/reduce_scatter | solution.py:94
  (83 shorter events, 38.2 us)
Async XLA Ops:
  7.2 501.3 %copy-start = (bf16[2048,512]{1,0:T(8,128)(2,1)S(1)}, bf16[2048,512]{1,0:T(8,128)(2,1)}, u32[]{:S(2)}) copy-start(bf16[2048,512]{1,0:T(8,128)(2,1)} %param.15) | copy-start | bytes 6291460
  7.2 693.7 %reduce-scatter.3.cloned.1.call-start = ((), (), s32[]{:S(2)}) async-start(), calls=%async_computation.2 | async-start | bytes 2621440 | tf_op jit(solution)/shard_map/reduce_scatter | solution.py:76
  22.3 3.2 copy-start.2
  31.8 3.7 copy-start.1
  35.6 1.2 copy-start.3
  37.7 2.2 copy-start.4
  42.9 3.2 copy-start.2
  52.7 3.7 copy-start.1
  56.5 1.2 copy-start.3
  58.6 2.1 copy-start.4
  63.8 3.2 copy-start.2
  73.6 3.7 copy-start.1
  77.3 1.2 copy-start.3
  79.5 2.1 copy-start.4
  84.7 3.2 copy-start.2
  94.4 3.7 copy-start.1
  98.2 1.2 copy-start.3
  100.3 2.2 copy-start.4
  508.4 1.6 copy-start.5
  510.0 2.7 copy-start.8
  510.0 189.9 %copy-start.6 = (bf16[512,128]{1,0:T(8,128)(2,1)S(1)}, bf16[512,128]{1,0:T(8,128)(2,1)}, u32[]{:S(2)}) copy-start(bf16[512,128]{1,0:T(8,128)(2,1)} %param.18) | copy-start | bytes 393220
  510.0 190.8 %copy-start.7 = (bf16[128,512]{1,0:T(8,128)(2,1)S(1)}, bf16[128,512]{1,0:T(8,128)(2,1)}, u32[]{:S(2)}) copy-start(bf16[128,512]{1,0:T(8,128)(2,1)} %param.19) | copy-start | bytes 393220
  512.7 228.4 %all-reduce.5.cloned.1.call-start = ((), (), s32[]{:S(2)}) async-start(), calls=%async_computation.4 | async-start | bytes 524288 | tf_op jit(solution)/shard_map/psum | solution.py:90
  702.9 428.5 %reduce-scatter.5.cloned.1.call-start = ((), (), s32[]{:S(2)}) async-start(), calls=%async_computation.3 | async-start | bytes 1064960 | tf_op jit(solution)/shard_map/reduce_scatter | solution.py:94
Sparse Core Ops, SparseCore 0:
  512.8 27.8 reduce-scatter.2
  703.0 38.0 all-reduce.4
  743.6 387.8 reduce-scatter.4
where the time goes:
time: 1140 us
  blocking collectives  591 us (52%)
  waiting for transfers between devices  423 us (37%)
  matrix products  58.8 us (5%)
  local copies, waits for them, and re-layouts  31.5 us (3%)
  other arithmetic  21.1 us (2%)
  between operations  13.8 us (1%)
    psum x1, blocking collectives, local(): key_sum, value_sum = lax.psum((key_total, value_total), 'seq')  404 us
    reduce_scatter x1, waiting for transfers between devices, local(): lax.psum_scatter(input_part, 'seq', scatter_dimension=0, tiled=True)  385 us
    all_gather x1, blocking collectives, local(): lax.all_gather(global_in, 'seq', axis=0, tiled=True)  187 us
    psum x1, waiting for transfers between devices, local(): lax.psum(back_part.astype(jnp.bfloat16), 'heads').astype(jnp.float32)  38.1 us
    dot_general x4, matrix products, attend(): jnp.einsum('hrg,rhd->ghd', weights_low, grad_block, preferred_element_typ...  26.1 us
  transfers between devices with their start and end apart: 3, of which 2 were waited for; matrix products, arithmetic and copies ran while one was open for 0% of the time, Pallas kernels for 0%

commit v1 on v0

v1 whole, which is shorter than its diff:
```python
import functools

import jax
import jax.numpy as jnp
from jax import lax
from jax.experimental import pallas as pl
from jax.experimental.pallas import tpu as pltpu
from jax.sharding import PartitionSpec as P

HD = 128
ROWS = 8
SCALE = HD ** (-0.5)
SCALE_LOG2E = SCALE * 1.4426950408889634
NT = (((1,), (1,)), ((), ()))
MESH = pl.DeviceIdType.MESH
F32 = jnp.float32
BF16 = jnp.bfloat16


def slope_of(pre):
    return (
        0.5 * (1.0 + lax.erf(pre * 0.7071067811865476))
        + pre * jnp.exp(-0.5 * pre * pre) * 0.3989422804014327
    )


def grid_of(seq):
    return {64: (4, 4, 4), 4: (2, 2, 1)}[seq]


def kernel(
    dims,
    q_hbm, k_hbm, v_hbm, g_hbm, kp_hbm, vp_hbm, gin_hbm, up_hbm, down_hbm,
    dq_hbm, gg_hbm,
    q, g, k, v, dq, wcat, up, down, gin,
    a1_send, a1_recv, state, a2_send, a2_recv, c_all,
    pre32, p_send, p_recv, slope, back32, d_send, d_recv, gated,
    e32, e_send, e_recv, gg,
    in_sem, w_sem, misc_sem, out_sem,
    wsend_sem, wrecv_sem, gsend_sem, grecv_sem,
    a1s_sem, a1r_sem, a2s_sem, a2r_sem, cs_sem, cr_sem,
    ps_sem, pr_sem, ds_sem, dr_sem, es_sem, er_sem,
):
    nx, nz, ny, nh = dims
    planes = nx * ny
    local_heads = q.shape[0]
    width = local_heads * HD
    half = planes * ROWS // 2
    hid = down_hbm.shape[0]
    s = lax.axis_index("seq")
    h = lax.axis_index("heads")
    x, z, y = s // (nz * ny), (s // ny) % nz, s % ny
    core = h % 2
    xy = x * ny + y
    zh = z * nh + h

    def seq_of(ax, az, ay):
        return (ax * nz + az) * ny + ay

    plane_peers = []
    for dx in range(nx):
        for dy in range(ny):
            if dx or dy:
                px, py = (x + dx) % nx, (y + dy) % ny
                plane_peers.append((px * ny + py, {"seq": seq_of(px, z, py), "heads": h}))
    column_peers = []
    for dz in range(nz):
        for dh in range(nh):
            if dz or dh:
                pz, ph = (z + dz) % nz, (h + dh) % nh
                column_peers.append((pz * nh + ph, {"seq": seq_of(x, pz, y), "heads": ph}))
    depth_peers = [{"seq": seq_of(x, (z + dz) % nz, y), "heads": h} for dz in range(1, nz)]
    partner = {"seq": s, "heads": h + 1 - 2 * core}
    across = {"seq": s, "heads": (h + 2) % nh}

    def remote(src, dst, send_sem, recv_sem, peer):
        return pltpu.make_async_remote_copy(
            src_ref=src, dst_ref=dst, send_sem=send_sem, recv_sem=recv_sem,
            device_id=peer, device_id_type=MESH,
        )

    def await_recv(ref, sem):
        pltpu.make_async_copy(ref, ref, sem).wait()

    barrier = pltpu.get_barrier_semaphore()
    for _, peer in plane_peers + column_peers:
        pl.semaphore_signal(barrier, inc=1, device_id=peer, device_id_type=MESH)

    loads = []
    for i in range(local_heads):
        cols = pl.ds(i * HD, HD)
        loads.append([
            pltpu.make_async_copy(src.at[:, cols], dst.at[i], in_sem.at[i, n])
            for n, (src, dst) in enumerate(((k_hbm, k), (q_hbm, q), (v_hbm, v), (g_hbm, g)))
        ])
    own_up = pltpu.make_async_copy(up_hbm, up.at[:, pl.ds(0, hid)], misc_sem.at[0])
    own_down = pltpu.make_async_copy(down_hbm, down.at[pl.ds(0, hid), :], misc_sem.at[1])
    own_gin = pltpu.make_async_copy(gin_hbm, gin.at[xy], misc_sem.at[2])
    for copy in loads[0]:
        copy.start()
    own_up.start()
    own_down.start()
    own_gin.start()
    for group in loads[1:]:
        for copy in group:
            copy.start()
    weight_loads = []
    for i in range(local_heads):
        cols = pl.ds(i * HD, HD)
        for n, src in enumerate((kp_hbm, vp_hbm)):
            weight_loads.append(
                pltpu.make_async_copy(src.at[:, cols], wcat.at[i, :, pl.ds(n * HD, HD)], w_sem.at[i, n])
            )
            weight_loads[-1].start()

    def attend(i):
        for copy in loads[i]:
            copy.wait()
        q_i, g_i, k_i, v_i = q[i], g[i], k[i], v[i]
        scores = lax.dot_general(k_i, q_i, NT, preferred_element_type=F32)
        weight_grad = lax.dot_general(v_i, g_i, NT, preferred_element_type=F32)
        top = jnp.max(scores, axis=0, keepdims=True)
        e = jnp.exp2((scores - top) * SCALE_LOG2E)
        inv = 1.0 / jnp.sum(e, axis=0, keepdims=True)
        weights = e * inv
        centre = jnp.sum(e * weight_grad, axis=0, keepdims=True) * inv
        score_grad = (weights * (weight_grad - centre)).astype(BF16)
        weights_low = weights.astype(BF16)
        query_grad = jnp.dot(k_i.T, score_grad, preferred_element_type=F32) * SCALE
        dq[i] = query_grad.astype(BF16).T
        dk = jnp.dot(score_grad, q_i, preferred_element_type=F32) * SCALE
        dv = jnp.dot(weights_low, g_i, preferred_element_type=F32)
        for ax in range(nx):
            for az in range(nz):
                for ay in range(ny):
                    r = seq_of(ax, az, ay) * ROWS
                    a1_send[i, ax * ny + ay, az] = jnp.concatenate(
                        [dk[r:r + ROWS], dv[r:r + ROWS]], axis=0
                    ).astype(BF16)

    def out_copy(i):
        return pltpu.make_async_copy(dq.at[i], dq_hbm.at[:, pl.ds(i * HD, HD)], out_sem.at[i])

    def a1_copies(i):
        return [
            remote(a1_send.at[i, pxy], a1_recv.at[i, n], a1s_sem.at[i], a1r_sem.at[i], peer)
            for n, (pxy, peer) in enumerate(plane_peers)
        ]

    def launch(i):
        out_copy(i).start()
        for copy in a1_copies(i):
            copy.start()

    def project(i):
        weight_loads[2 * i].wait()
        weight_loads[2 * i + 1].wait()
        await_recv(a1_recv.at[i], a1r_sem.at[i])
        total = a1_send[i, xy].astype(F32)
        for n in range(planes - 1):
            total = total + a1_recv[i, n].astype(F32)
        low = jnp.concatenate(
            [total[:, :ROWS].reshape(nz * ROWS, HD), total[:, ROWS:].reshape(nz * ROWS, HD)], axis=1
        ).astype(BF16)
        return lax.dot_general(low, wcat[i], NT, preferred_element_type=F32)

    attend(0)

    pl.semaphore_wait(barrier, len(plane_peers) + len(column_peers))
    own_gin.wait()
    gin_copies = [
        remote(gin.at[xy], gin.at[xy], gsend_sem, grecv_sem, peer) for _, peer in plane_peers
    ]
    own_up.wait()
    own_down.wait()
    weight_copies = []
    for n, peer in enumerate(depth_peers):
        span = pl.ds((n + 1) * hid, hid)
        weight_copies.append(
            remote(up.at[:, pl.ds(0, hid)], up.at[:, span], wsend_sem.at[0], wrecv_sem.at[0], peer)
        )
        weight_copies.append(
            remote(down.at[pl.ds(0, hid), :], down.at[span, :], wsend_sem.at[1], wrecv_sem.at[1], peer)
        )
    for copy in gin_copies + weight_copies:
        copy.start()
    launch(0)

    for i in range(1, local_heads):
        attend(i)
        launch(i)
        part = project(i - 1)
        state[...] = part if i == 1 else state[...] + part

    await_recv(gin.at[pl.ds(0, planes - 1)], grecv_sem)
    await_recv(up.at[:, pl.ds(hid, (nz - 1) * hid)], wrecv_sem.at[0])
    rows_in = gin[...].astype(F32).reshape(planes * ROWS, width).astype(BF16)
    pre = jnp.dot(rows_in, up[...], preferred_element_type=F32)
    pre32[0] = pre[:half]
    pre32[1] = pre[half:]
    p_send[0] = pre32[1 - core].astype(BF16)
    p_first = remote(p_send.at[0], p_recv.at[0], ps_sem.at[0], pr_sem.at[0], partner)
    p_first.start()
    p_first.wait_recv()
    pre_half = pre32[core] + p_recv[0].astype(F32)
    p_send[1] = pre_half.astype(BF16)
    p_second = remote(p_send.at[1], p_recv.at[1], ps_sem.at[1], pr_sem.at[1], across)
    p_second.start()
    p_second.wait_recv()
    slope[...] = slope_of(pre_half + p_recv[1].astype(F32))

    total = state[...] + project(local_heads - 1)
    for az in range(nz):
        for ah in range(nh):
            piece = total[az * ROWS:(az + 1) * ROWS, ah * width:(ah + 1) * width]
            a2_send[az * nh + ah] = piece.astype(BF16)
    a2_copies = [
        remote(a2_send.at[pzh], a2_recv.at[n], a2s_sem, a2r_sem, peer)
        for n, (pzh, peer) in enumerate(column_peers)
    ]
    for copy in a2_copies:
        copy.start()
    await_recv(a2_recv, a2r_sem)
    own_state = a2_send[zh].astype(F32)
    for n in range(nz * nh - 1):
        own_state = own_state + a2_recv[n].astype(F32)

    c_all[xy] = own_state.astype(BF16)
    c_copies = [remote(c_all.at[xy], c_all.at[xy], cs_sem, cr_sem, peer) for _, peer in plane_peers]
    for copy in c_copies:
        copy.start()
    await_recv(down.at[pl.ds(hid, (nz - 1) * hid), :], wrecv_sem.at[1])
    await_recv(c_all.at[pl.ds(0, planes - 1)], cr_sem)
    rows_state = c_all[...].astype(F32).reshape(planes * ROWS, width).astype(BF16)
    back = lax.dot_general(rows_state, down[...], NT, preferred_element_type=F32)
    back32[0] = back[:half]
    back32[1] = back[half:]
    d_send[0] = back32[1 - core].astype(BF16)
    d_first = remote(d_send.at[0], d_recv.at[0], ds_sem.at[0], dr_sem.at[0], partner)
    d_first.start()
    d_first.wait_recv()
    back_half = back32[core] + d_recv[0].astype(F32)
    d_send[1] = back_half.astype(BF16)
    d_second = remote(d_send.at[1], d_recv.at[1], ds_sem.at[1], dr_sem.at[1], across)
    d_second.start()
    d_second.wait_recv()
    gated[core] = (slope[...] * (back_half + d_recv[1].astype(F32))).astype(BF16)
    d_third = remote(gated.at[core], gated.at[core], ds_sem.at[2], dr_sem.at[2], partner)
    d_third.start()
    d_third.wait_recv()

    full = jnp.concatenate([gated[0], gated[1]], axis=0)
    out = lax.dot_general(full, up[...], NT, preferred_element_type=F32)
    out = out.reshape(planes, ROWS, width)
    e32[...] = out
    e_send[...] = out.astype(BF16)
    e_copies = [
        remote(e_send.at[pxy], e_recv.at[n], es_sem, er_sem, peer)
        for n, (pxy, peer) in enumerate(plane_peers)
    ]
    for copy in e_copies:
        copy.start()
    await_recv(e_recv, er_sem)
    result = own_state + e32[xy]
    for n in range(planes - 1):
        result = result + e_recv[n].astype(F32)
    gg[...] = result
    last = pltpu.make_async_copy(gg, gg_hbm, misc_sem.at[3])
    last.start()

    for i in range(local_heads):
        out_copy(i).wait()
        await_recv(a1_recv.at[i], a1s_sem.at[i])
    await_recv(gin.at[pl.ds(0, planes - 1)], gsend_sem)
    await_recv(up.at[:, pl.ds(hid, (nz - 1) * hid)], wsend_sem.at[0])
    await_recv(down.at[pl.ds(hid, (nz - 1) * hid), :], wsend_sem.at[1])
    p_first.wait_send()
    p_second.wait_send()
    await_recv(a2_recv, a2s_sem)
    await_recv(c_all.at[pl.ds(0, planes - 1)], cs_sem)
    d_first.wait_send()
    d_second.wait_send()
    d_third.wait_send()
    await_recv(e_recv, es_sem)
    last.wait()


def local(queries, keys, values, out_grad, key_proj, value_proj, global_in, up_proj, down_proj):
    seq, nh = lax.axis_size("seq"), lax.axis_size("heads")
    nx, nz, ny = grid_of(seq)
    planes = nx * ny
    tokens, width = queries.shape
    globs = keys.shape[0]
    heads = width // HD
    model = key_proj.shape[0]
    hid = down_proj.shape[0]
    half = planes * ROWS // 2
    all_hid = nz * hid
    dma, vmem = pltpu.SemaphoreType.DMA, pltpu.VMEM
    anywhere = pl.BlockSpec(memory_space=pl.ANY)
    return pl.pallas_call(
        functools.partial(kernel, (nx, nz, ny, nh)),
        out_shape=(
            jax.ShapeDtypeStruct((tokens, width), BF16),
            jax.ShapeDtypeStruct((ROWS, width), F32),
        ),
        in_specs=[anywhere] * 9,
        out_specs=(anywhere, anywhere),
        scratch_shapes=[
            vmem((heads, tokens, HD), BF16),
            vmem((heads, tokens, HD), BF16),
            vmem((heads, globs, HD), BF16),
            vmem((heads, globs, HD), BF16),
            vmem((heads, tokens, HD), BF16),
            vmem((heads, model, 2 * HD), BF16),
            vmem((width, all_hid), BF16),
            vmem((all_hid, width), BF16),
            vmem((planes, ROWS, width), BF16),
            vmem((heads, planes, nz, 2 * ROWS, HD), BF16),
            vmem((heads, planes - 1, nz, 2 * ROWS, HD), BF16),
            vmem((nz * ROWS, model), F32),
            vmem((nz * nh, ROWS, width), BF16),
            vmem((nz * nh - 1, ROWS, width), BF16),
            vmem((planes, ROWS, width), BF16),
            vmem((2, half, all_hid), F32),
            vmem((2, half, all_hid), BF16),
            vmem((2, half, all_hid), BF16),
            vmem((half, all_hid), F32),
            vmem((2, half, all_hid), F32),
            vmem((2, half, all_hid), BF16),
            vmem((2, half, all_hid), BF16),
            vmem((2, half, all_hid), BF16),
            vmem((planes, ROWS, width), F32),
            vmem((planes, ROWS, width), BF16),
            vmem((planes - 1, ROWS, width), BF16),
            vmem((ROWS, width), F32),
            dma((heads, 4)), dma((heads, 2)), dma((4,)), dma((heads,)),
            dma((2,)), dma((2,)), dma, dma,
            dma((heads,)), dma((heads,)), dma, dma, dma, dma,
            dma((2,)), dma((2,)), dma((3,)), dma((3,)), dma, dma,
        ],
        compiler_params=pltpu.CompilerParams(
            collective_id=0, has_side_effects=True, vmem_limit_bytes=60 * 1024 * 1024
        ),
    )(queries, keys, values, out_grad, key_proj, value_proj, global_in, up_proj, down_proj)


def solution(mesh):
    placed = (
        P("seq", "heads"),
        P(None, "heads"),
        P(None, "heads"),
        P("seq", "heads"),
        P(None, "heads"),
        P(None, "heads"),
        P("seq", "heads"),
        P("heads", "seq"),
        P("seq", "heads"),
    )
    return jax.shard_map(
        local,
        mesh=mesh,
        in_specs=placed,
        out_specs=(P("seq", "heads"), P("seq", "heads")),
        check_vma=False,
    )
```

time: 1140 us -> 66.6 us (0.06)
  the two profiles are of different devices: /device:TPU:0 before, /device:TPU:1 now
where the time goes in v1:
time: 66.6 us; the launch traced here: 66.5 us
  Pallas kernels  62.2 us (93%)
  local copies, waits for them, and re-layouts  3.66 us (5%)
    pallas_call x1, Pallas kernels, local(): pl.pallas_call(functools.partial(kernel, (nx, nz, ny, nh)), out_shape=(ja...  62.2 us
    unnamed x4, local copies, waits for them, and re-layouts  3.66 us

profile of v1, /device:TPU:1, one launch (start us, length us, event | category | flops | bytes accessed | tf_op | source)
XLA Modules:
  0.0 66.5 jit_solution(12420659237880001938)
XLA Ops:
  0.6 62.2 %shard_map.104 = (bf16[2048,512]{1,0:T(8,128)(2,1)}, f32[8,512]{1,0:T(8,128)}) custom-call(bf16[2048,512]{1,0:T(8,128)(2,1)} %q_hbm.1, bf16[512,512]{1,0:T(8,128)(2,1)} %k_hbm.1, bf16[512,512]{1,0:T(8,128)(2,1)} %v_hbm.1, bf16[2048,512]{1,0:T(8,128)(2,1)} %g_hbm.1, bf16[2048,512]{1,0:T(8,128)(2,1)} %kp_hbm.1, bf16[2048,512]{1,0:T(8,128)(2,1)} %vp_hbm.1, ...), custom_call_target="tpu_custom_call" | custom-call | tf_op jit(solution)/shard_map/pallas_call | solution.py:301
  62.8 0.0 copy-start
  62.8 3.0 %copy.13 = bf16[2048,512]{1,0:T(8,128)(2,1)} copy(bf16[2048,512]{1,0:T(8,128)(2,1)} %get-tuple-element.4) | data formatting | bytes 4194304
  65.9 0.0 copy-done
  65.9 0.6 copy.14
Async XLA Ops:
  62.8 3.1 %copy-start = (f32[8,512]{1,0:T(8,128)S(1)}, f32[8,512]{1,0:T(8,128)}, u32[]{:S(2)}) copy-start(f32[8,512]{1,0:T(8,128)} %get-tuple-element.5) | copy-start | bytes 49156
